TPU v7x, 256 devices: a whole 4x4x8 slice. The times are simulated.
256 devices in a mesh: blk: 8 (over x_lo, y), freq: 32 (over x_hi, z, core).
Axes of the slice: x: 4 (x_hi: 2, x_lo: 2; x = x_hi * 2 + x_lo), y: 4, z: 8, core: 2. Of those that a mesh axis runs over, the one named last changes fastest.
Arguments:
- spectra: bfloat16 [2048, 2, 4096], P('blk', None, 'freq'), may hold values from -180 to 180
- pair_first: int32 [8, 8, 2048], P('blk'), may hold values from 0 to 255
- pair_second: int32 [8, 8, 2048], P('blk'), may hold values from 0 to 255
- pair_bin: int32 [8, 8, 2048], P('blk'), may hold values from 0 to 63, as said below
- bin_owner: int32 [64], replicated, may hold values from 0 to 7, as said below
Outputs:
- correlation: float32 [4096, 128], P('freq', 'blk')
Inputs may be any that keep to these rules, and one draw needn't show every extreme that they name: Each list pair_bin[a, r] is nondecreasing along its last dimension, starts with 0 and ends with 63. `bin_owner`: each block index owns at most 16 bins, and some index owns exactly 16.
All inputs are finite; a program needn't handle non-finite values.
Results may differ from a plain program's by a relative error of at most 0.0049.
Values may be sent and summed in bfloat16 or wider, within the bound.
No kernel may reach another device: no remote copies, remote signals or barrier semaphores. Data moves between devices by JAX's collectives and lax.ppermute only.
A program may use at most 64 MiB of HBM per device.

v0:
```python
import math
import jax
import jax.numpy as jnp
from jax import lax
from jax.sharding import PartitionSpec as P

F = 4096
NB = 64
PAIRS = 2048


def from_behind(x, axis, by):
    devices = lax.axis_size(axis)
    return lax.ppermute(x, axis, [(i, (i + by) % devices) for i in range(devices)])


def cross_stack(total, white, remote, first_rows, second_rows, bin_rows):
    left = white[first_rows].astype(jnp.float32)
    right = remote[second_rows].astype(jnp.float32)
    real_part = left[:, 0] * right[:, 0] + left[:, 1] * right[:, 1]
    imag_part = left[:, 1] * right[:, 0] - left[:, 0] * right[:, 1]
    cross = jnp.stack([real_part, imag_part], 1).astype(jnp.bfloat16)
    onehot = (bin_rows[None, :] == jnp.arange(NB, dtype=jnp.int32)[:, None]).astype(jnp.bfloat16)
    flat = cross.reshape(cross.shape[0], -1)
    return total + jnp.dot(onehot, flat, preferred_element_type=jnp.float32)


def lag_block(lag_rows, freq_rows, piece):
    phase = (lag_rows[:, None] * freq_rows[None, :] % F).astype(jnp.float32) * (2.0 * math.pi / F)
    line = jnp.dot(jnp.cos(phase), piece[:, 0, :].T, precision=lax.Precision.HIGHEST)
    return line - jnp.dot(jnp.sin(phase), piece[:, 1, :].T, precision=lax.Precision.HIGHEST)


def on_device(spectra, pair_first, pair_second, pair_bin, bin_owner):
    blocks = lax.axis_size("blk")
    freq_dev = spectra.shape[2]
    values = spectra.astype(jnp.float32)
    power = lax.psum(jnp.sum(values * values, axis=(1, 2)), "freq")
    rms = jnp.sqrt(power / (2 * F) + 1e-06)
    white = (values / rms[:, None, None]).astype(jnp.bfloat16)
    total = jnp.zeros((NB, 2 * freq_dev), jnp.float32)
    remote = white
    for step_count in range(blocks):
        if step_count > 0:
            remote = from_behind(remote, "blk", 1)
        total = cross_stack(
            total,
            white,
            remote,
            pair_first[0, step_count],
            pair_second[0, step_count],
            pair_bin[0, step_count],
        )
    partial_stack = total.reshape(NB, 2, freq_dev)
    slots_each = 2 * NB // blocks
    bins = jnp.arange(NB, dtype=jnp.int32)
    same = bin_owner[:, None] == bin_owner[None, :]
    lower = bins[None, :] < bins[:, None]
    rank = jnp.sum((same & lower).astype(jnp.int32), axis=1)
    slot = bin_owner * slots_each + rank
    totals = lax.psum(partial_stack, "blk")
    mine = lax.axis_index("blk")
    wanted = mine * slots_each + jnp.arange(slots_each, dtype=jnp.int32)
    select = (slot[None, :] == wanted[:, None]).astype(jnp.float32)
    owned = jnp.einsum("sb,bcf->scf", select, totals, precision=lax.Precision.HIGHEST)
    freq_index = lax.axis_index("freq")
    scale = (F * PAIRS * blocks * blocks / NB) ** (-0.5)
    lag_rows = jnp.arange(freq_dev * lax.axis_size("freq"), dtype=jnp.int32)
    freq_rows = freq_index * freq_dev + jnp.arange(freq_dev, dtype=jnp.int32)
    line = lax.psum_scatter(
        lag_block(lag_rows, freq_rows, owned), "freq", scatter_dimension=0, tiled=True
    )
    return line * scale


def solution(mesh):
    return jax.shard_map(
        on_device,
        mesh=mesh,
        in_specs=(
            P("blk", None, "freq"),
            P("blk", None, None),
            P("blk", None, None),
            P("blk", None, None),
            P(),
        ),
        out_specs=P("freq", "blk"),
        check_vma=False,
    )
```

profile of v0, /device:TPU:8, one launch (start us, length us, event | category | flops | bytes accessed | tf_op | source)
XLA Modules:
  0.0 524.1 jit_solution(14951603235629611911)
XLA Ops:
  8.5 72.8 %psum.14 = f32[256]{0:T(256)S(1)} all-reduce(f32[256]{0:T(256)S(1)} %fusion.29), channel_id=1, replica_groups=mesh['blk'=8,'freq'=32] {'freq'}, use_global_device_ids=true, to_apply=%region_2.0 | all-reduce | flops 256 | bytes 2048 | tf_op jit(solution)/shard_map/psum | solution.py:38
  85.5 7.1 %gather_fusion = bf16[2048,2,128]{2,1,0:T(2,128)(2,1)S(1)} fusion(bf16[256,2,128]{2,1,0:T(2,128)(2,1)S(1)} %fusion.30, s32[2048]{0:T(1024)S(1)} %broadcast_clamp_fusion.15), kind=kCustom, calls=%fused_computation | custom fusion | bytes 2105344 | tf_op jit(solution)/shard_map/gather | solution.py:18
  93.5 7.0 %gather_fusion.1 = bf16[2048,2,128]{2,1,0:T(2,128)(2,1)S(1)} fusion(bf16[256,2,128]{2,1,0:T(2,128)(2,1)S(1)} %fusion.30, s32[2048]{0:T(1024)S(1)} %broadcast_clamp_fusion.14), kind=kCustom, calls=%fused_computation.1 | custom fusion | bytes 2105344 | tf_op jit(solution)/shard_map/gather | solution.py:19
  109.1 7.0 %gather_fusion.2 = bf16[2048,2,128]{2,1,0:T(2,128)(2,1)S(1)} fusion(bf16[256,2,128]{2,1,0:T(2,128)(2,1)S(1)} %fusion.30, s32[2048]{0:T(1024)S(1)} %broadcast_clamp_fusion.13), kind=kCustom, calls=%fused_computation.2 | custom fusion | bytes 2105344 | tf_op jit(solution)/shard_map/gather | solution.py:18
  117.9 7.0 %gather_fusion.4 = bf16[2048,2,128]{2,1,0:T(2,128)(2,1)S(1)} fusion(bf16[256,2,128]{2,1,0:T(2,128)(2,1)S(1)} %fusion.30, s32[2048]{0:T(1024)S(1)} %broadcast_clamp_fusion.11), kind=kCustom, calls=%fused_computation.4 | custom fusion | bytes 2105344 | tf_op jit(solution)/shard_map/gather | solution.py:18
  126.7 7.1 %gather_fusion.6 = bf16[2048,2,128]{2,1,0:T(2,128)(2,1)S(1)} fusion(bf16[256,2,128]{2,1,0:T(2,128)(2,1)S(1)} %fusion.30, s32[2048]{0:T(1024)S(1)} %broadcast_clamp_fusion.9), kind=kCustom, calls=%fused_computation.6 | custom fusion | bytes 2105344 | tf_op jit(solution)/shard_map/gather | solution.py:18
  135.6 7.0 %gather_fusion.8 = bf16[2048,2,128]{2,1,0:T(2,128)(2,1)S(1)} fusion(bf16[256,2,128]{2,1,0:T(2,128)(2,1)S(1)} %fusion.30, s32[2048]{0:T(1024)S(1)} %broadcast_clamp_fusion.7), kind=kCustom, calls=%fused_computation.8 | custom fusion | bytes 2105344 | tf_op jit(solution)/shard_map/gather | solution.py:18
  144.4 7.1 %gather_fusion.10 = bf16[2048,2,128]{2,1,0:T(2,128)(2,1)S(1)} fusion(bf16[256,2,128]{2,1,0:T(2,128)(2,1)S(1)} %fusion.30, s32[2048]{0:T(1024)S(1)} %broadcast_clamp_fusion.5), kind=kCustom, calls=%fused_computation.10 | custom fusion | bytes 2105344 | tf_op jit(solution)/shard_map/gather | solution.py:18
  153.2 7.1 %gather_fusion.12 = bf16[2048,2,128]{2,1,0:T(2,128)(2,1)S(1)} fusion(bf16[256,2,128]{2,1,0:T(2,128)(2,1)S(1)} %fusion.30, s32[2048]{0:T(1024)S(1)} %broadcast_clamp_fusion.3), kind=kCustom, calls=%fused_computation.12 | custom fusion | bytes 2105344 | tf_op jit(solution)/shard_map/gather | solution.py:18
  162.0 7.0 %gather_fusion.14 = bf16[2048,2,128]{2,1,0:T(2,128)(2,1)S(1)} fusion(bf16[256,2,128]{2,1,0:T(2,128)(2,1)S(1)} %fusion.30, s32[2048]{0:T(1024)S(1)} %broadcast_clamp_fusion.1), kind=kCustom, calls=%fused_computation.14 | custom fusion | bytes 2105344 | tf_op jit(solution)/shard_map/gather | solution.py:18
  169.9 7.0 %gather_fusion.3 = bf16[2048,2,128]{2,1,0:T(2,128)(2,1)S(1)} fusion(bf16[256,2,128]{2,1,0:T(2,128)(2,1)S(1)} %collective-permute-done, s32[2048]{0:T(1024)S(1)} %broadcast_clamp_fusion.12), kind=kCustom, calls=%fused_computation.3 | custom fusion | bytes 2105344 | tf_op jit(solution)/shard_map/gather | solution.py:19
  189.5 7.0 %gather_fusion.5 = bf16[2048,2,128]{2,1,0:T(2,128)(2,1)S(1)} fusion(bf16[256,2,128]{2,1,0:T(2,128)(2,1)S(1)} %collective-permute-done.1, s32[2048]{0:T(1024)S(1)} %broadcast_clamp_fusion.10), kind=kCustom, calls=%fused_computation.5 | custom fusion | bytes 2105344 | tf_op jit(solution)/shard_map/gather | solution.py:19
  209.5 7.0 %gather_fusion.7 = bf16[2048,2,128]{2,1,0:T(2,128)(2,1)S(1)} fusion(bf16[256,2,128]{2,1,0:T(2,128)(2,1)S(1)} %collective-permute-done.2, s32[2048]{0:T(1024)S(1)} %broadcast_clamp_fusion.8), kind=kCustom, calls=%fused_computation.7 | custom fusion | bytes 2105344 | tf_op jit(solution)/shard_map/gather | solution.py:19
  231.0 7.4 %gather_fusion.9 = bf16[2048,2,128]{2,1,0:T(2,128)(2,1)S(1)} fusion(bf16[256,2,128]{2,1,0:T(2,128)(2,1)S(1)} %collective-permute-done.3, s32[2048]{0:T(1024)S(1)} %broadcast_clamp_fusion.6), kind=kCustom, calls=%fused_computation.9 | custom fusion | bytes 2105344 | tf_op jit(solution)/shard_map/gather | solution.py:19
  246.9 6.1 %collective-permute-done.4 = bf16[256,2,128]{2,1,0:T(2,128)(2,1)S(1)} collective-permute-done((bf16[256,2,128]{2,1,0:T(2,128)(2,1)S(1)}, bf16[256,2,128]{2,1,0:T(2,128)(2,1)S(1)}, u32[]{:S(2)}, u32[]{:S(2)}) %collective-permute-start.4) | collective-permute-done | bytes 131104 | tf_op jit(solution)/shard_map/ppermute | solution.py:14
  253.0 7.0 %gather_fusion.11 = bf16[2048,2,128]{2,1,0:T(2,128)(2,1)S(1)} fusion(bf16[256,2,128]{2,1,0:T(2,128)(2,1)S(1)} %collective-permute-done.4, s32[2048]{0:T(1024)S(1)} %broadcast_clamp_fusion.4), kind=kCustom, calls=%fused_computation.11 | custom fusion | bytes 2105344 | tf_op jit(solution)/shard_map/gather | solution.py:19
  268.4 6.1 %collective-permute-done.5 = bf16[256,2,128]{2,1,0:T(2,128)(2,1)S(1)} collective-permute-done((bf16[256,2,128]{2,1,0:T(2,128)(2,1)S(1)}, bf16[256,2,128]{2,1,0:T(2,128)(2,1)S(1)}, u32[]{:S(2)}, u32[]{:S(2)}) %collective-permute-start.5) | collective-permute-done | bytes 131104 | tf_op jit(solution)/shard_map/ppermute | solution.py:14
  274.5 7.1 %gather_fusion.13 = bf16[2048,2,128]{2,1,0:T(2,128)(2,1)S(1)} fusion(bf16[256,2,128]{2,1,0:T(2,128)(2,1)S(1)} %collective-permute-done.5, s32[2048]{0:T(1024)S(1)} %broadcast_clamp_fusion.2), kind=kCustom, calls=%fused_computation.13 | custom fusion | bytes 2105344 | tf_op jit(solution)/shard_map/gather | solution.py:19
  290.1 6.1 %collective-permute-done.6 = bf16[256,2,128]{2,1,0:T(2,128)(2,1)S(1)} collective-permute-done((bf16[256,2,128]{2,1,0:T(2,128)(2,1)S(1)}, bf16[256,2,128]{2,1,0:T(2,128)(2,1)S(1)}, u32[]{:S(2)}, u32[]{:S(2)}) %collective-permute-start.6) | collective-permute-done | bytes 131104 | tf_op jit(solution)/shard_map/ppermute | solution.py:14
  296.3 7.0 %gather_fusion.15 = bf16[2048,2,128]{2,1,0:T(2,128)(2,1)S(1)} fusion(bf16[256,2,128]{2,1,0:T(2,128)(2,1)S(1)} %collective-permute-done.6, s32[2048]{0:T(1024)S(1)} %broadcast_clamp_fusion), kind=kCustom, calls=%fused_computation.15 | custom fusion | bytes 2105344 | tf_op jit(solution)/shard_map/gather | solution.py:19
  310.9 72.5 %all-reduce.2.cloned.1.call-done = f32[64,2,128]{2,0,1:T(8,128)} async-done(((f32[64,2,128]{2,0,1:T(8,128)}), f32[64,2,128]{2,0,1:T(8,128)}) %all-reduce.2.cloned.1.call-update) | async-done | bytes 65552 | tf_op jit(solution)/shard_map/psum | solution.py:61
  384.4 9.5 %fusion.4 = f32[4096,16]{0,1:T(8,128)S(1)} fusion(s32[128]{0:T(128)S(1)} %iota_add_fusion.1, f32[16,2,128]{2,0,1:T(8,128)S(1)} %fusion.40), kind=kOutput, calls=%fused_computation.24 | convolution fusion | flops 108003328 | bytes 270848 | tf_op jit(solution)/shard_map/dot_general | solution.py:30
  393.9 11.2 %convolution_subtract_fusion = f32[4096,16]{0,1:T(8,128)} fusion(f32[4096,16]{0,1:T(8,128)S(1)} %fusion.4, s32[128]{0:T(128)S(1)} %iota_add_fusion.1, f32[16,2,128]{2,0,1:T(8,128)S(1)} %fusion.40), kind=kOutput, calls=%fused_computation.16 | convolution fusion | flops 108068864 | bytes 532992 | tf_op jit(solution)/shard_map/dot_general | solution.py:31
  405.1 110.6 %reduce-scatter.2.cloned.1.call-done = f32[128,16]{0,1:T(8,128)} async-done(((f32[4096,16]{0,1:T(8,128)}), f32[128,16]{0,1:T(8,128)}) %reduce-scatter.2.cloned.1.call-update) | async-done | bytes 8208 | tf_op jit(solution)/shard_map/reduce_scatter | solution.py:70
  (126 shorter events, 101.6 us)
Async XLA Ops:
  6.5 376.8 %all-reduce.2.cloned.1.call-start = ((), (), s32[]{:S(2)}) async-start(), calls=%async_computation.1 | async-start | bytes 131072 | tf_op jit(solution)/shard_map/psum | solution.py:61
  82.5 87.3 %collective-permute-start = (bf16[256,2,128]{2,1,0:T(2,128)(2,1)S(1)}, bf16[256,2,128]{2,1,0:T(2,128)(2,1)S(1)}, u32[]{:S(2)}, u32[]{:S(2)}) collective-permute-start(bf16[256,2,128]{2,1,0:T(2,128)(2,1)S(1)} %fusion.30), channel_id=1, source_target_pairs={{0,32},{32,64},{64,96},{96,128},{128,160},{160,192},{192,224},{224... | collective-permute-start | bytes 393224 | tf_op jit(solution)/shard_map/ppermute | solution.py:14
  100.6 1.6 copy-start.13
  181.8 4.1 copy-start.12
  181.8 4.1 copy-start.14
  184.4 5.0 collective-permute-start.1
  201.4 3.9 copy-start.11
  201.4 3.9 copy-start.15
  203.9 5.6 %collective-permute-start.2 = (bf16[256,2,128]{2,1,0:T(2,128)(2,1)S(1)}, bf16[256,2,128]{2,1,0:T(2,128)(2,1)S(1)}, u32[]{:S(2)}, u32[]{:S(2)}) collective-permute-start(bf16[256,2,128]{2,1,0:T(2,128)(2,1)S(1)} %collective-permute-done.1), channel_id=1, source_target_pairs={{0,32},{32,64},{64,96},{96,128},{128,160},{160,192},{192,224},{224... | collective-permute-start | bytes 393224 | tf_op jit(solution)/shard_map/ppermute | solution.py:14
  216.6 1.6 copy-start.3
  221.4 3.4 copy-start.10
  221.4 3.4 copy-start.16
  223.9 7.1 %collective-permute-start.3 = (bf16[256,2,128]{2,1,0:T(2,128)(2,1)S(1)}, bf16[256,2,128]{2,1,0:T(2,128)(2,1)S(1)}, u32[]{:S(2)}, u32[]{:S(2)}) collective-permute-start(bf16[256,2,128]{2,1,0:T(2,128)(2,1)S(1)} %collective-permute-done.2), channel_id=1, source_target_pairs={{0,32},{32,64},{64,96},{96,128},{128,160},{160,192},{192,224},{224... | collective-permute-start | bytes 393224 | tf_op jit(solution)/shard_map/ppermute | solution.py:14
  238.5 1.6 copy-start.2
  243.4 2.6 copy-start.9
  243.4 2.6 copy-start.17
  245.8 7.2 %collective-permute-start.4 = (bf16[256,2,128]{2,1,0:T(2,128)(2,1)S(1)}, bf16[256,2,128]{2,1,0:T(2,128)(2,1)S(1)}, u32[]{:S(2)}, u32[]{:S(2)}) collective-permute-start(bf16[256,2,128]{2,1,0:T(2,128)(2,1)S(1)} %collective-permute-done.3), channel_id=1, source_target_pairs={{0,32},{32,64},{64,96},{96,128},{128,160},{160,192},{192,224},{224... | collective-permute-start | bytes 393224 | tf_op jit(solution)/shard_map/ppermute | solution.py:14
  264.9 2.6 copy-start.8
  264.9 2.6 copy-start.18
  267.4 7.2 %collective-permute-start.5 = (bf16[256,2,128]{2,1,0:T(2,128)(2,1)S(1)}, bf16[256,2,128]{2,1,0:T(2,128)(2,1)S(1)}, u32[]{:S(2)}, u32[]{:S(2)}) collective-permute-start(bf16[256,2,128]{2,1,0:T(2,128)(2,1)S(1)} %collective-permute-done.4), channel_id=1, source_target_pairs={{0,32},{32,64},{64,96},{96,128},{128,160},{160,192},{192,224},{224... | collective-permute-start | bytes 393224 | tf_op jit(solution)/shard_map/ppermute | solution.py:14
  286.5 2.7 copy-start.19
  288.9 7.3 %collective-permute-start.6 = (bf16[256,2,128]{2,1,0:T(2,128)(2,1)S(1)}, bf16[256,2,128]{2,1,0:T(2,128)(2,1)S(1)}, u32[]{:S(2)}, u32[]{:S(2)}) collective-permute-start(bf16[256,2,128]{2,1,0:T(2,128)(2,1)S(1)} %collective-permute-done.5), channel_id=1, source_target_pairs={{0,32},{32,64},{64,96},{96,128},{128,160},{160,192},{192,224},{224... | collective-permute-start | bytes 393224 | tf_op jit(solution)/shard_map/ppermute | solution.py:14
  307.4 2.5 copy-start.20
  310.8 205.0 %reduce-scatter.2.cloned.1.call-start = ((), (), s32[]{:S(2)}) async-start(), calls=%async_computation.2 | async-start | bytes 270336 | tf_op jit(solution)/shard_map/reduce_scatter | solution.py:70
  (6 other events, 8.1 us)
Sparse Core Ops, SparseCore 0:
  310.9 72.3 all-reduce.1
  405.3 110.4 reduce-scatter.1
where the time goes:
time: 534 us; the launch traced here: 524 us
  waiting for transfers between devices  213 us (40%)
  local copies, waits for them, and re-layouts  119 us (22%)
  blocking collectives  72.8 us (14%)
  other arithmetic  70.4 us (13%)
  matrix products  28.5 us (5%)
  between operations  14.4 us (3%)
  starting transfers between devices  5.95 us (1%)
    reduce_scatter x1, waiting for transfers between devices, on_device(): lax.psum_scatter(lag_block(lag_rows, freq_rows, owned), 'freq', scatter_d...  111 us
    psum x1, blocking collectives, on_device(): power = lax.psum(jnp.sum(values * values, axis=(1, 2)), 'freq')  72.8 us
    psum x1, waiting for transfers between devices, on_device(): totals = lax.psum(partial_stack, 'blk')  72.5 us
    gather x8, local copies, waits for them, and re-layouts, cross_stack(): right = remote[second_rows].astype(jnp.float32)  56.8 us
    gather x8, local copies, waits for them, and re-layouts, cross_stack(): left = white[first_rows].astype(jnp.float32)  56.4 us
    ppermute x7, waiting for transfers between devices, from_behind(): lax.ppermute(x, axis, [(i, (i + by) % devices) for i in range(devices)])  29.6 us
    another operation x8, other arithmetic  26.3 us
    another operation x8, other arithmetic, cross_stack(): cross = jnp.stack([real_part, imag_part], 1).astype(jnp.bfloat16)  19.6 us
  transfers between devices with their start and end apart: 9, of which 8 were waited for; matrix products, arithmetic and copies ran while one was open for 17% of the time, Pallas kernels for 0%

commit v1 on v0

--- a/solution.py
+++ b/solution.py
@@ -35,7 +35,9 @@
     blocks = lax.axis_size("blk")
     freq_dev = spectra.shape[2]
     values = spectra.astype(jnp.float32)
-    power = lax.psum(jnp.sum(values * values, axis=(1, 2)), "freq")
+    own = jnp.sum(values * values, axis=(1, 2))
+    pieces = lax.all_gather(own, "freq")
+    power = jnp.sum(pieces, axis=0)
     rms = jnp.sqrt(power / (2 * F) + 1e-06)
     white = (values / rms[:, None, None]).astype(jnp.bfloat16)
     total = jnp.zeros((NB, 2 * freq_dev), jnp.float32)

time: 534 us -> 500 us (0.936); the launches traced: 524 us -> 497 us
  blocking collectives: 72.8 us -> 44.8 us
    psum x1 -> x0, blocking collectives: 72.8 us -> none  [on_device(): power = lax.psum(jnp.sum(values * values, axis=(1, 2)), 'freq')]
    all_gather x0 -> x1, blocking collectives: none -> 44.8 us  [on_device(): pieces = lax.all_gather(own, 'freq')]
  transfers between devices with their start and end apart: 9 -> 9, of which waited for: 8 -> 8; matrix products, arithmetic and copies ran while one was open for 17% -> 18% of each run, Pallas kernels for 0% -> 0%
where the time goes in v1:
time: 500 us; the launch traced here: 497 us
  waiting for transfers between devices  214 us (43%)
  local copies, waits for them, and re-layouts  119 us (24%)
  other arithmetic  70.4 us (14%)
  blocking collectives  44.8 us (9%)
  matrix products  28.5 us (6%)
  between operations  14.4 us (3%)
  starting transfers between devices  6.1 us (1%)
    reduce_scatter x1, waiting for transfers between devices, on_device(): lax.psum_scatter(lag_block(lag_rows, freq_rows, owned), 'freq', scatter_d...  111 us
    psum x1, waiting for transfers between devices, on_device(): totals = lax.psum(partial_stack, 'blk')  72.4 us
    gather x8, local copies, waits for them, and re-layouts, cross_stack(): right = remote[second_rows].astype(jnp.float32)  56.8 us
    gather x8, local copies, waits for them, and re-layouts, cross_stack(): left = white[first_rows].astype(jnp.float32)  56.4 us
    all_gather x1, blocking collectives, on_device(): pieces = lax.all_gather(own, 'freq')  44.8 us
    ppermute x7, waiting for transfers between devices, from_behind(): lax.ppermute(x, axis, [(i, (i + by) % devices) for i in range(devices)])  30.4 us
    another operation x8, other arithmetic  26.3 us
    another operation x8, other arithmetic, cross_stack(): cross = jnp.stack([real_part, imag_part], 1).astype(jnp.bfloat16)  19.6 us
  transfers between devices with their start and end apart: 9, of which 8 were waited for; matrix products, arithmetic and copies ran while one was open for 18% of the time, Pallas kernels for 0%

profile of v1, /device:TPU:8, one launch (start us, length us, event | category | flops | bytes accessed | tf_op | source)
XLA Modules:
  0.0 497.1 jit_solution(13551304964917014355)
XLA Ops:
  8.5 44.8 %all-gather.1 = f32[32,1,256]{2,1,0:T(1,128)S(1)} all-gather(f32[1,1,256]{2,1,0:T(1,128)S(1)} %bitcast.137), channel_id=2, replica_groups=mesh['blk'=8,'freq'=32] {'freq'}, dimensions={0}, use_global_device_ids=true | all-gather | bytes 33792 | tf_op jit(solution)/shard_map/all_gather | solution.py:39
  58.0 7.1 %gather_fusion = bf16[2048,2,128]{2,1,0:T(2,128)(2,1)S(1)} fusion(bf16[256,2,128]{2,1,0:T(2,128)(2,1)S(1)} %fusion.30, s32[2048]{0:T(1024)S(1)} %broadcast_clamp_fusion.15), kind=kCustom, calls=%fused_computation | custom fusion | bytes 2105344 | tf_op jit(solution)/shard_map/gather | solution.py:18
  66.0 7.0 %gather_fusion.1 = bf16[2048,2,128]{2,1,0:T(2,128)(2,1)S(1)} fusion(bf16[256,2,128]{2,1,0:T(2,128)(2,1)S(1)} %fusion.30, s32[2048]{0:T(1024)S(1)} %broadcast_clamp_fusion.14), kind=kCustom, calls=%fused_computation.1 | custom fusion | bytes 2105344 | tf_op jit(solution)/shard_map/gather | solution.py:19
  81.6 7.0 %gather_fusion.2 = bf16[2048,2,128]{2,1,0:T(2,128)(2,1)S(1)} fusion(bf16[256,2,128]{2,1,0:T(2,128)(2,1)S(1)} %fusion.30, s32[2048]{0:T(1024)S(1)} %broadcast_clamp_fusion.13), kind=kCustom, calls=%fused_computation.2 | custom fusion | bytes 2105344 | tf_op jit(solution)/shard_map/gather | solution.py:18
  90.4 7.0 %gather_fusion.4 = bf16[2048,2,128]{2,1,0:T(2,128)(2,1)S(1)} fusion(bf16[256,2,128]{2,1,0:T(2,128)(2,1)S(1)} %fusion.30, s32[2048]{0:T(1024)S(1)} %broadcast_clamp_fusion.11), kind=kCustom, calls=%fused_computation.4 | custom fusion | bytes 2105344 | tf_op jit(solution)/shard_map/gather | solution.py:18
  99.2 7.1 %gather_fusion.6 = bf16[2048,2,128]{2,1,0:T(2,128)(2,1)S(1)} fusion(bf16[256,2,128]{2,1,0:T(2,128)(2,1)S(1)} %fusion.30, s32[2048]{0:T(1024)S(1)} %broadcast_clamp_fusion.9), kind=kCustom, calls=%fused_computation.6 | custom fusion | bytes 2105344 | tf_op jit(solution)/shard_map/gather | solution.py:18
  108.1 7.0 %gather_fusion.8 = bf16[2048,2,128]{2,1,0:T(2,128)(2,1)S(1)} fusion(bf16[256,2,128]{2,1,0:T(2,128)(2,1)S(1)} %fusion.30, s32[2048]{0:T(1024)S(1)} %broadcast_clamp_fusion.7), kind=kCustom, calls=%fused_computation.8 | custom fusion | bytes 2105344 | tf_op jit(solution)/shard_map/gather | solution.py:18
  116.9 7.1 %gather_fusion.10 = bf16[2048,2,128]{2,1,0:T(2,128)(2,1)S(1)} fusion(bf16[256,2,128]{2,1,0:T(2,128)(2,1)S(1)} %fusion.30, s32[2048]{0:T(1024)S(1)} %broadcast_clamp_fusion.5), kind=kCustom, calls=%fused_computation.10 | custom fusion | bytes 2105344 | tf_op jit(solution)/shard_map/gather | solution.py:18
  125.7 7.1 %gather_fusion.12 = bf16[2048,2,128]{2,1,0:T(2,128)(2,1)S(1)} fusion(bf16[256,2,128]{2,1,0:T(2,128)(2,1)S(1)} %fusion.30, s32[2048]{0:T(1024)S(1)} %broadcast_clamp_fusion.3), kind=kCustom, calls=%fused_computation.12 | custom fusion | bytes 2105344 | tf_op jit(solution)/shard_map/gather | solution.py:18
  134.5 7.0 %gather_fusion.14 = bf16[2048,2,128]{2,1,0:T(2,128)(2,1)S(1)} fusion(bf16[256,2,128]{2,1,0:T(2,128)(2,1)S(1)} %fusion.30, s32[2048]{0:T(1024)S(1)} %broadcast_clamp_fusion.1), kind=kCustom, calls=%fused_computation.14 | custom fusion | bytes 2105344 | tf_op jit(solution)/shard_map/gather | solution.py:18
  142.4 7.0 %gather_fusion.3 = bf16[2048,2,128]{2,1,0:T(2,128)(2,1)S(1)} fusion(bf16[256,2,128]{2,1,0:T(2,128)(2,1)S(1)} %collective-permute-done, s32[2048]{0:T(1024)S(1)} %broadcast_clamp_fusion.12), kind=kCustom, calls=%fused_computation.3 | custom fusion | bytes 2105344 | tf_op jit(solution)/shard_map/gather | solution.py:19
  162.5 7.0 %gather_fusion.5 = bf16[2048,2,128]{2,1,0:T(2,128)(2,1)S(1)} fusion(bf16[256,2,128]{2,1,0:T(2,128)(2,1)S(1)} %collective-permute-done.1, s32[2048]{0:T(1024)S(1)} %broadcast_clamp_fusion.10), kind=kCustom, calls=%fused_computation.5 | custom fusion | bytes 2105344 | tf_op jit(solution)/shard_map/gather | solution.py:19
  182.5 7.0 %gather_fusion.7 = bf16[2048,2,128]{2,1,0:T(2,128)(2,1)S(1)} fusion(bf16[256,2,128]{2,1,0:T(2,128)(2,1)S(1)} %collective-permute-done.2, s32[2048]{0:T(1024)S(1)} %broadcast_clamp_fusion.8), kind=kCustom, calls=%fused_computation.7 | custom fusion | bytes 2105344 | tf_op jit(solution)/shard_map/gather | solution.py:19
  204.1 7.4 %gather_fusion.9 = bf16[2048,2,128]{2,1,0:T(2,128)(2,1)S(1)} fusion(bf16[256,2,128]{2,1,0:T(2,128)(2,1)S(1)} %collective-permute-done.3, s32[2048]{0:T(1024)S(1)} %broadcast_clamp_fusion.6), kind=kCustom, calls=%fused_computation.9 | custom fusion | bytes 2105344 | tf_op jit(solution)/shard_map/gather | solution.py:19
  219.9 6.1 %collective-permute-done.4 = bf16[256,2,128]{2,1,0:T(2,128)(2,1)S(1)} collective-permute-done((bf16[256,2,128]{2,1,0:T(2,128)(2,1)S(1)}, bf16[256,2,128]{2,1,0:T(2,128)(2,1)S(1)}, u32[]{:S(2)}, u32[]{:S(2)}) %collective-permute-start.4) | collective-permute-done | bytes 131104 | tf_op jit(solution)/shard_map/ppermute | solution.py:14
  226.0 7.0 %gather_fusion.11 = bf16[2048,2,128]{2,1,0:T(2,128)(2,1)S(1)} fusion(bf16[256,2,128]{2,1,0:T(2,128)(2,1)S(1)} %collective-permute-done.4, s32[2048]{0:T(1024)S(1)} %broadcast_clamp_fusion.4), kind=kCustom, calls=%fused_computation.11 | custom fusion | bytes 2105344 | tf_op jit(solution)/shard_map/gather | solution.py:19
  241.4 6.1 %collective-permute-done.5 = bf16[256,2,128]{2,1,0:T(2,128)(2,1)S(1)} collective-permute-done((bf16[256,2,128]{2,1,0:T(2,128)(2,1)S(1)}, bf16[256,2,128]{2,1,0:T(2,128)(2,1)S(1)}, u32[]{:S(2)}, u32[]{:S(2)}) %collective-permute-start.5) | collective-permute-done | bytes 131104 | tf_op jit(solution)/shard_map/ppermute | solution.py:14
  247.6 7.1 %gather_fusion.13 = bf16[2048,2,128]{2,1,0:T(2,128)(2,1)S(1)} fusion(bf16[256,2,128]{2,1,0:T(2,128)(2,1)S(1)} %collective-permute-done.5, s32[2048]{0:T(1024)S(1)} %broadcast_clamp_fusion.2), kind=kCustom, calls=%fused_computation.13 | custom fusion | bytes 2105344 | tf_op jit(solution)/shard_map/gather | solution.py:19
  263.2 6.1 %collective-permute-done.6 = bf16[256,2,128]{2,1,0:T(2,128)(2,1)S(1)} collective-permute-done((bf16[256,2,128]{2,1,0:T(2,128)(2,1)S(1)}, bf16[256,2,128]{2,1,0:T(2,128)(2,1)S(1)}, u32[]{:S(2)}, u32[]{:S(2)}) %collective-permute-start.6) | collective-permute-done | bytes 131104 | tf_op jit(solution)/shard_map/ppermute | solution.py:14
  269.3 7.0 %gather_fusion.15 = bf16[2048,2,128]{2,1,0:T(2,128)(2,1)S(1)} fusion(bf16[256,2,128]{2,1,0:T(2,128)(2,1)S(1)} %collective-permute-done.6, s32[2048]{0:T(1024)S(1)} %broadcast_clamp_fusion), kind=kCustom, calls=%fused_computation.15 | custom fusion | bytes 2105344 | tf_op jit(solution)/shard_map/gather | solution.py:19
  283.9 72.4 %all-reduce.2.cloned.1.call-done = f32[64,2,128]{2,0,1:T(8,128)} async-done(((f32[64,2,128]{2,0,1:T(8,128)}), f32[64,2,128]{2,0,1:T(8,128)}) %all-reduce.2.cloned.1.call-update) | async-done | bytes 65552 | tf_op jit(solution)/shard_map/psum | solution.py:63
  357.4 9.5 %fusion.4 = f32[4096,16]{0,1:T(8,128)S(1)} fusion(s32[128]{0:T(128)S(1)} %iota_add_fusion.1, f32[16,2,128]{2,0,1:T(8,128)S(1)} %fusion.40), kind=kOutput, calls=%fused_computation.24 | convolution fusion | flops 108003328 | bytes 270848 | tf_op jit(solution)/shard_map/dot_general | solution.py:30
  366.9 11.2 %convolution_subtract_fusion = f32[4096,16]{0,1:T(8,128)} fusion(f32[4096,16]{0,1:T(8,128)S(1)} %fusion.4, s32[128]{0:T(128)S(1)} %iota_add_fusion.1, f32[16,2,128]{2,0,1:T(8,128)S(1)} %fusion.40), kind=kOutput, calls=%fused_computation.16 | convolution fusion | flops 108068864 | bytes 532992 | tf_op jit(solution)/shard_map/dot_general | solution.py:31
  378.1 110.6 %reduce-scatter.2.cloned.1.call-done = f32[128,16]{0,1:T(8,128)} async-done(((f32[4096,16]{0,1:T(8,128)}), f32[128,16]{0,1:T(8,128)}) %reduce-scatter.2.cloned.1.call-update) | async-done | bytes 8208 | tf_op jit(solution)/shard_map/reduce_scatter | solution.py:72
  (127 shorter events, 102.6 us)
Async XLA Ops:
  6.5 349.8 %all-reduce.2.cloned.1.call-start = ((), (), s32[]{:S(2)}) async-start(), calls=%async_computation.1 | async-start | bytes 131072 | tf_op jit(solution)/shard_map/psum | solution.py:63
  54.6 87.8 %collective-permute-start = (bf16[256,2,128]{2,1,0:T(2,128)(2,1)S(1)}, bf16[256,2,128]{2,1,0:T(2,128)(2,1)S(1)}, u32[]{:S(2)}, u32[]{:S(2)}) collective-permute-start(bf16[256,2,128]{2,1,0:T(2,128)(2,1)S(1)} %fusion.30), channel_id=1, source_target_pairs={{0,32},{32,64},{64,96},{96,128},{128,160},{160,192},{192,224},{224... | collective-permute-start | bytes 393224 | tf_op jit(solution)/shard_map/ppermute | solution.py:14
  73.1 1.6 copy-start.13
  149.4 1.6 copy-start.5
  154.3 4.0 copy-start.12
  154.3 4.0 copy-start.14
  157.0 5.5 %collective-permute-start.1 = (bf16[256,2,128]{2,1,0:T(2,128)(2,1)S(1)}, bf16[256,2,128]{2,1,0:T(2,128)(2,1)S(1)}, u32[]{:S(2)}, u32[]{:S(2)}) collective-permute-start(bf16[256,2,128]{2,1,0:T(2,128)(2,1)S(1)} %collective-permute-done), channel_id=1, source_target_pairs={{0,32},{32,64},{64,96},{96,128},{128,160},{160,192},{192,224},{224... | collective-permute-start | bytes 393224 | tf_op jit(solution)/shard_map/ppermute | solution.py:14
  174.4 3.8 copy-start.11
  174.4 3.8 copy-start.15
  176.9 5.6 %collective-permute-start.2 = (bf16[256,2,128]{2,1,0:T(2,128)(2,1)S(1)}, bf16[256,2,128]{2,1,0:T(2,128)(2,1)S(1)}, u32[]{:S(2)}, u32[]{:S(2)}) collective-permute-start(bf16[256,2,128]{2,1,0:T(2,128)(2,1)S(1)} %collective-permute-done.1), channel_id=1, source_target_pairs={{0,32},{32,64},{64,96},{96,128},{128,160},{160,192},{192,224},{224... | collective-permute-start | bytes 393224 | tf_op jit(solution)/shard_map/ppermute | solution.py:14
  194.5 3.3 copy-start.10
  194.5 3.3 copy-start.16
  196.9 7.1 %collective-permute-start.3 = (bf16[256,2,128]{2,1,0:T(2,128)(2,1)S(1)}, bf16[256,2,128]{2,1,0:T(2,128)(2,1)S(1)}, u32[]{:S(2)}, u32[]{:S(2)}) collective-permute-start(bf16[256,2,128]{2,1,0:T(2,128)(2,1)S(1)} %collective-permute-done.2), channel_id=1, source_target_pairs={{0,32},{32,64},{64,96},{96,128},{128,160},{160,192},{192,224},{224... | collective-permute-start | bytes 393224 | tf_op jit(solution)/shard_map/ppermute | solution.py:14
  216.4 2.6 copy-start.9
  216.4 2.6 copy-start.17
  218.8 7.2 %collective-permute-start.4 = (bf16[256,2,128]{2,1,0:T(2,128)(2,1)S(1)}, bf16[256,2,128]{2,1,0:T(2,128)(2,1)S(1)}, u32[]{:S(2)}, u32[]{:S(2)}) collective-permute-start(bf16[256,2,128]{2,1,0:T(2,128)(2,1)S(1)} %collective-permute-done.3), channel_id=1, source_target_pairs={{0,32},{32,64},{64,96},{96,128},{128,160},{160,192},{192,224},{224... | collective-permute-start | bytes 393224 | tf_op jit(solution)/shard_map/ppermute | solution.py:14
  233.1 1.6 copy-start.1
  237.9 2.6 copy-start.8
  238.0 2.6 copy-start.18
  240.4 7.2 %collective-permute-start.5 = (bf16[256,2,128]{2,1,0:T(2,128)(2,1)S(1)}, bf16[256,2,128]{2,1,0:T(2,128)(2,1)S(1)}, u32[]{:S(2)}, u32[]{:S(2)}) collective-permute-start(bf16[256,2,128]{2,1,0:T(2,128)(2,1)S(1)} %collective-permute-done.4), channel_id=1, source_target_pairs={{0,32},{32,64},{64,96},{96,128},{128,160},{160,192},{192,224},{224... | collective-permute-start | bytes 393224 | tf_op jit(solution)/shard_map/ppermute | solution.py:14
  259.5 2.7 copy-start.19
  262.0 7.3 %collective-permute-start.6 = (bf16[256,2,128]{2,1,0:T(2,128)(2,1)S(1)}, bf16[256,2,128]{2,1,0:T(2,128)(2,1)S(1)}, u32[]{:S(2)}, u32[]{:S(2)}) collective-permute-start(bf16[256,2,128]{2,1,0:T(2,128)(2,1)S(1)} %collective-permute-done.5), channel_id=1, source_target_pairs={{0,32},{32,64},{64,96},{96,128},{128,160},{160,192},{192,224},{224... | collective-permute-start | bytes 393224 | tf_op jit(solution)/shard_map/ppermute | solution.py:14
  280.4 2.5 copy-start.20
  283.8 204.9 %reduce-scatter.2.cloned.1.call-start = ((), (), s32[]{:S(2)}) async-start(), calls=%async_computation.2 | async-start | bytes 270336 | tf_op jit(solution)/shard_map/reduce_scatter | solution.py:72
  (6 other events, 8.1 us)
Sparse Core Ops, SparseCore 0:
  284.0 72.3 all-reduce.1
  378.3 110.4 reduce-scatter.1
